TPU v7x, 256 devices: a whole 4x4x8 slice. The times are simulated.
256 devices in a mesh: dp: 16 (over x, y), head: 16 (over z, core).
Axes of the slice: x: 4, y: 4, z: 8, core: 2. Of those that a mesh axis runs over, the one named last changes fastest.
Arguments:
- query: bfloat16 [32768, 12288], P(('dp', 'head')), may hold values from -160 to 160
- latent: bfloat16 [32768, 576], P(('dp', 'head')), may hold values from -6 to 6
- d_attn: bfloat16 [32768, 8192], P(('dp', 'head')), may hold values from -6 to 6
- w_kv: bfloat16 [512, 16384], P('dp', 'head'), may hold values from -0.25 to 0.25
- doc_lengths: int32 [16, 10], P('dp'), may hold values from 1 to 384, 2048 in all within a row
Outputs:
- d_query: bfloat16 [32768, 12288], P(('dp', 'head'))
- d_latent: float32 [32768, 576], P(('dp', 'head'))
- d_w_kv: float32 [512, 16384], P('dp', 'head')
Inputs may be any that keep to these rules, and one draw needn't show every extreme that they name: `doc_lengths`: row g lists the lengths of the 10 documents of data group g; they sum to 2048, and the longest of each row is exactly 384.
All inputs are finite; a program needn't handle non-finite values.
Results may differ from a plain program's by a relative error of at most 0.025.
Values may be sent and summed in bfloat16 or wider, within the bound.
No kernel may reach another device: no remote copies, remote signals or barrier semaphores. Data moves between devices by JAX's collectives and lax.ppermute only.
A program may use at most 128 MiB of HBM per device.

v0:
```python
import math
import jax
import jax.numpy as jnp
from jax import lax
from jax.sharding import PartitionSpec as P

NOPE = 128
ROPE = 64
VDIM = 128
KV_RANK = 512
DOC_MAX = 384
QB = 128
masked_score = -1e30


def document_index(lengths_row, count):
    ends = jnp.cumsum(lengths_row)
    positions = jnp.arange(count, dtype=jnp.int32)
    return jnp.sum((positions[:, None] >= ends[None, :]).astype(jnp.int32), axis=1)


def attend_backward(queries, keys_padded, values_padded, grads_out, doc_padded, block, window):
    seq_len = queries.shape[0]
    reach = window - block
    scale = 1.0 / math.sqrt(queries.shape[2])
    blocks = seq_len // block

    def one_block(carry, index):
        grad_keys, grad_values = carry
        first = index * block
        query_rows = lax.dynamic_slice_in_dim(queries, first, block, 0)
        key_rows = lax.dynamic_slice_in_dim(keys_padded, first, window, 0)
        value_rows = lax.dynamic_slice_in_dim(values_padded, first, window, 0)
        out_rows = lax.dynamic_slice_in_dim(grads_out, first, block, 0)
        query_doc = lax.dynamic_slice_in_dim(doc_padded, first + reach, block, 0)
        key_doc = lax.dynamic_slice_in_dim(doc_padded, first, window, 0)
        query_pos = jnp.arange(block, dtype=jnp.int32) + reach
        key_pos = jnp.arange(window, dtype=jnp.int32)
        allowed = (key_pos[None, :] <= query_pos[:, None]) & (
            key_doc[None, :] == query_doc[:, None]
        )
        scores = (
            jnp.einsum("qhd,khd->hqk", query_rows, key_rows, preferred_element_type=jnp.float32)
            * scale
        )
        scores = jnp.where(allowed[None], scores, masked_score)
        top = jnp.max(scores, axis=2, keepdims=True)
        weights = jnp.exp(scores - top)
        probs = weights / jnp.sum(weights, axis=2, keepdims=True)
        probs_low = probs.astype(jnp.bfloat16)
        attn_out = jnp.einsum(
            "hqk,khd->qhd", probs_low, value_rows, preferred_element_type=jnp.float32
        )
        delta = jnp.sum(out_rows.astype(jnp.float32) * attn_out, axis=2)
        dprob = jnp.einsum("qhd,khd->hqk", out_rows, value_rows, preferred_element_type=jnp.float32)
        dscore_low = (probs * (dprob - jnp.transpose(delta)[:, :, None])).astype(jnp.bfloat16)
        grad_query = (
            jnp.einsum("hqk,khd->qhd", dscore_low, key_rows, preferred_element_type=jnp.float32)
            * scale
        )
        grad_key_rows = (
            jnp.einsum("hqk,qhd->khd", dscore_low, query_rows, preferred_element_type=jnp.float32)
            * scale
        )
        grad_value_rows = jnp.einsum(
            "hqk,qhd->khd", probs_low, out_rows, preferred_element_type=jnp.float32
        )
        grad_keys = lax.dynamic_update_slice_in_dim(
            grad_keys,
            lax.dynamic_slice_in_dim(grad_keys, first, window, 0) + grad_key_rows,
            first,
            0,
        )
        grad_values = lax.dynamic_update_slice_in_dim(
            grad_values,
            lax.dynamic_slice_in_dim(grad_values, first, window, 0) + grad_value_rows,
            first,
            0,
        )
        return ((grad_keys, grad_values), grad_query.astype(jnp.bfloat16))

    start_keys = jnp.zeros(keys_padded.shape, jnp.float32)
    start_values = jnp.zeros(values_padded.shape, jnp.float32)
    (grad_keys, grad_values), grad_queries = lax.scan(
        one_block, (start_keys, start_values), jnp.arange(blocks, dtype=jnp.int32)
    )
    grad_queries = grad_queries.reshape(seq_len, queries.shape[1] * queries.shape[2])
    return (grad_keys[reach:], grad_values[reach:], grad_queries)


def local(query, latent, d_attn, w_kv, doc_lengths):
    group_size = lax.axis_size("head")
    own_tokens = query.shape[0]
    seq_len = own_tokens * group_size
    head_count = w_kv.shape[1] // (NOPE + VDIM)
    queries, grads_out = (
        lax.all_to_all(query, "head", split_axis=1, concat_axis=0, tiled=True),
        lax.all_to_all(d_attn, "head", split_axis=1, concat_axis=0, tiled=True),
    )
    latents = lax.all_gather(latent, "head", axis=0, tiled=True)
    compressed = latents[:, :KV_RANK]
    whole_weight = lax.all_gather(w_kv, "dp", axis=0, tiled=True)
    kv_up = jnp.dot(compressed, whole_weight, preferred_element_type=jnp.float32)
    kv_up = kv_up.astype(jnp.bfloat16).reshape(seq_len, head_count, NOPE + VDIM)
    rotary = jnp.broadcast_to(latents[:, None, KV_RANK:], (seq_len, head_count, ROPE))
    keys = jnp.concatenate([kv_up[:, :, :NOPE], rotary], axis=2)
    keys_padded = jnp.concatenate(
        [jnp.zeros((DOC_MAX, head_count, NOPE + ROPE), jnp.bfloat16), keys], axis=0
    )
    values_padded = jnp.concatenate(
        [jnp.zeros((DOC_MAX, head_count, VDIM), jnp.bfloat16), kv_up[:, :, NOPE:]], axis=0
    )
    doc_ids = document_index(doc_lengths[0], seq_len)
    doc_padded = jnp.concatenate([jnp.full((DOC_MAX,), -1, jnp.int32), doc_ids])
    grad_keys, grad_values, grad_queries = attend_backward(
        queries.reshape(seq_len, head_count, NOPE + ROPE),
        keys_padded,
        values_padded,
        grads_out.reshape(seq_len, head_count, VDIM),
        doc_padded,
        QB,
        DOC_MAX + QB,
    )
    returned = lax.all_to_all(grad_queries, "head", split_axis=0, concat_axis=1, tiled=True)
    grad_kv = jnp.concatenate([grad_keys[:, :, :NOPE], grad_values], axis=2).astype(jnp.bfloat16)
    grad_kv = grad_kv.reshape(seq_len, head_count * (NOPE + VDIM))
    grad_weight = lax.psum_scatter(
        lax.dot_general(
            compressed, grad_kv, (((0,), (0,)), ((), ())), preferred_element_type=jnp.float32
        ).astype(jnp.bfloat16),
        "dp",
        scatter_dimension=0,
        tiled=True,
    ).astype(jnp.float32)
    grad_compressed = lax.dot_general(
        grad_kv, whole_weight, (((1,), (1,)), ((), ())), preferred_element_type=jnp.float32
    )
    head_terms = jnp.concatenate([grad_compressed, jnp.sum(grad_keys[:, :, NOPE:], axis=1)], axis=1)
    summed = lax.psum(head_terms.astype(jnp.bfloat16), "head").astype(jnp.float32)
    grad_latent = lax.dynamic_slice_in_dim(
        summed, lax.axis_index("head") * own_tokens, own_tokens, 0
    )
    return (returned, grad_latent, grad_weight)


def solution(mesh):
    placed = (
        P(("dp", "head"), None),
        P(("dp", "head"), None),
        P(("dp", "head"), None),
        P("dp", "head"),
        P("dp", None),
    )
    return jax.shard_map(
        local,
        mesh=mesh,
        in_specs=placed,
        out_specs=(P(("dp", "head"), None), P(("dp", "head"), None), P("dp", "head")),
        check_vma=False,
    )
```

profile of v0, /device:TPU:2, one launch (start us, length us, event | category | flops | bytes accessed | tf_op | source)
XLA Modules:
  0.0 728.3 jit_solution(18205139117940249030)
XLA Ops:
  7.2 4.1 copy.52
  11.2 8.6 %all-to-all-start.1 = ((bf16[128,16,512]{0,2,1:T(8,128)(2,1)}), bf16[128,16,512]{0,2,1:T(8,128)(2,1)S(1)}, u32[]{:S(2)}, u32[]{:S(2)}) async-start(bf16[128,16,512]{0,2,1:T(8,128)(2,1)} %bitcast.74), calls=%async_computation.1 | async-start | bytes 4194304 | tf_op jit(solution)/shard_map/all_to_all | solution.py:98
  21.3 4.6 copy.50
  25.9 43.1 %all-to-all-done.1 = bf16[128,16,512]{0,2,1:T(8,128)(2,1)S(1)} async-done(((bf16[128,16,512]{0,2,1:T(8,128)(2,1)}), bf16[128,16,512]{0,2,1:T(8,128)(2,1)S(1)}, u32[]{:S(2)}, u32[]{:S(2)}) %all-to-all-start.1) | async-done | bytes 2097184 | tf_op jit(solution)/shard_map/all_to_all | solution.py:98
  70.4 4.7 all-to-all-start
  75.4 4.3 copy.53
  79.7 4.2 reshape.117
  83.9 74.2 %all-gather.3.cloned.1.call-done = bf16[2048,576]{0,1:T(8,128)(2,1)} async-done(((bf16[128,576]{0,1:T(8,128)(2,1)}), bf16[2048,576]{0,1:T(8,128)(2,1)}) %all-gather.3.cloned.1.call-update) | async-done | bytes 2359312 | tf_op jit(solution)/shard_map/all_gather | solution.py:100
  158.1 4.2 convolution_convert_fusion
  165.0 4.0 copy.66
  168.9 3.4 concatenate.23
  174.4 3.7 copy.51
  178.1 5.8 reshape.113
  183.9 3.5 broadcast_in_dim.54
  190.0 266.0 %while.16 = (s32[]{:T(128)}, f32[2432,4,192]{0,2,1:T(8,128)}, f32[2432,4,128]{0,2,1:T(8,128)}, bf16[16,128,4,192]{1,3,2,0:T(8,128)(2,1)}, s32[16]{0:T(128)S(1)},...) while((s32[]{:T(128)}, f32[2432,4,192]{0,2,1:T(8,128)}, ...), condition=%wide.region_6.7_spmd, body=%wide.region_2.6_spmd.sunk | while | flops 711002240 | bytes 15294786 | solution.py:84
  201.1 3.3 fusion.128
  317.5 3.3 fusion.128
  417.2 3.3 fusion.128
  455.9 4.7 copy.56
  460.6 6.1 all-to-all-start.2
  479.1 6.3 fusion.67
  487.7 142.7 %all-reduce.5.cloned.1.call-done = bf16[2048,576]{0,1:T(8,128)(2,1)} async-done(((bf16[2048,576]{0,1:T(8,128)(2,1)}), bf16[2048,576]{0,1:T(8,128)(2,1)}) %all-reduce.5.cloned.1.call-update) | async-done | bytes 2359312 | tf_op jit(solution)/shard_map/psum | solution.py:139
  632.0 80.5 %reduce-scatter.4.cloned.1.call-done = bf16[32,1024]{1,0:T(8,128)(2,1)} async-done(((bf16[512,1024]{1,0:T(8,128)(2,1)}), bf16[32,1024]{1,0:T(8,128)(2,1)}) %reduce-scatter.4.cloned.1.call-update) | async-done | bytes 65552
  717.1 4.6 copy.58
  (248 shorter events, 276.1 us)
Async XLA Ops:
  11.2 57.8 %all-to-all-start.1 = ((bf16[128,16,512]{0,2,1:T(8,128)(2,1)}), bf16[128,16,512]{0,2,1:T(8,128)(2,1)S(1)}, u32[]{:S(2)}, u32[]{:S(2)}) async-start(bf16[128,16,512]{0,2,1:T(8,128)(2,1)} %bitcast.74), calls=%async_computation.1 | async-start | bytes 4194304 | tf_op jit(solution)/shard_map/all_to_all | solution.py:98
  19.8 64.1 %all-gather.5.cloned.1.call-start = ((), (), s32[]{:S(2)}) async-start(), calls=%async_computation.5 | async-start | bytes 1114112 | tf_op jit(solution)/shard_map/all_gather | solution.py:102
  20.6 137.6 %all-gather.3.cloned.1.call-start = ((), (), s32[]{:S(2)}) async-start(), calls=%async_computation.4 | async-start | bytes 2506752 | tf_op jit(solution)/shard_map/all_gather | solution.py:100
  69.0 1.4 copy-start
  69.0 6.0 copy-start.4
  70.4 104.0 %all-to-all-start = ((bf16[128,16,768]{0,2,1:T(8,128)(2,1)}), bf16[128,16,768]{0,2,1:T(8,128)(2,1)S(1)}, u32[]{:S(2)}, u32[]{:S(2)}) async-start(bf16[128,16,768]{0,2,1:T(8,128)(2,1)} %bitcast.7), calls=%async_computation | async-start | bytes 6291456 | tf_op jit(solution)/shard_map/all_to_all | solution.py:97
  168.9 3.4 slice-start
  168.9 3.5 copy-start.1
  460.6 253.7 %all-to-all-start.2 = ((bf16[16,128,768]{2,1,0:T(8,128)(2,1)}), bf16[16,128,768]{2,1,0:T(8,128)(2,1)S(1)}, u32[]{:S(2)}, u32[]{:S(2)}) async-start(bf16[16,128,768]{2,1,0:T(8,128)(2,1)} %copy.56), calls=%async_computation.2 | async-start | bytes 6291456 | tf_op jit(solution)/shard_map/all_to_all | solution.py:124
  466.7 163.7 %all-reduce.5.cloned.1.call-start = ((), (), s32[]{:S(2)}) async-start(), calls=%async_computation.6 | async-start | bytes 4718592 | tf_op jit(solution)/shard_map/psum | solution.py:139
  473.7 1.2 copy-start.3
  474.3 3.0 copy-start.2
  479.0 233.5 %reduce-scatter.4.cloned.1.call-start = ((), (), s32[]{:S(2)}) async-start(), calls=%async_computation.7 | async-start | bytes 1114112
Sparse Core Ops, SparseCore 0:
  23.1 48.6 all-gather.4
  73.5 84.6 all-gather.2
  479.2 151.1 all-reduce.4
  633.7 78.7 reduce-scatter.3
where the time goes:
time: 733 us; the launch traced here: 728 us
  waiting for transfers between devices  342 us (47%)
  matrix products  237 us (32%)
  local copies, waits for them, and re-layouts  94.5 us (13%)
  starting transfers between devices  19.7 us (3%)
  between operations  13.9 us (2%)
  loops' own time  11.1 us (2%)
  other arithmetic  10.1 us (1%)
    psum x1, waiting for transfers between devices, local(): lax.psum(head_terms.astype(jnp.bfloat16), 'head').astype(jnp.float32)  143 us
    unnamed x5, waiting for transfers between devices  81.9 us
    all_gather x1, waiting for transfers between devices, local(): latents = lax.all_gather(latent, 'head', axis=0, tiled=True)  74.2 us
    dot_general x16, matrix products, one_block(): jnp.einsum('hqk,qhd->khd', probs_low, out_rows, preferred_element_type=jn...  52.8 us
    dot_general x16, matrix products, one_block(): jnp.einsum('hqk,qhd->khd', dscore_low, query_rows, preferred_element_type...  49.7 us
    all_to_all x1, waiting for transfers between devices, local(): lax.all_to_all(d_attn, 'head', split_axis=1, concat_axis=0, tiled=True)  43.1 us
    dot_general x16, matrix products, one_block(): jnp.einsum('hqk,khd->qhd', dscore_low, key_rows, preferred_element_type=j...  34.8 us
    dot_general x16, matrix products, one_block(): jnp.einsum('hqk,khd->qhd', probs_low, value_rows, preferred_element_type=...  34.8 us
  transfers between devices with their start and end apart: 7, of which 4 were waited for; matrix products, arithmetic and copies ran while one was open for 7% of the time, Pallas kernels for 0%

commit v1 on v0

--- a/solution.py
+++ b/solution.py
@@ -97,7 +97,8 @@
         lax.all_to_all(query, "head", split_axis=1, concat_axis=0, tiled=True),
         lax.all_to_all(d_attn, "head", split_axis=1, concat_axis=0, tiled=True),
     )
-    latents = lax.all_gather(latent, "head", axis=0, tiled=True)
+    y1 = jnp.stack([latent] * lax.axis_size("head"))
+    latents = jnp.concatenate(lax.all_to_all(y1, "head", 0, 0), 0)
     compressed = latents[:, :KV_RANK]
     whole_weight = lax.all_gather(w_kv, "dp", axis=0, tiled=True)
     kv_up = jnp.dot(compressed, whole_weight, preferred_element_type=jnp.float32)

time: 733 us -> 765 us (1.044)
  blocking collectives: 0 us -> 58.3 us
  waiting for transfers between devices: 342 us -> 317 us
    all_gather x1 -> x0, waiting for transfers between devices: 74.2 us -> none  [local(): latents = lax.all_gather(latent, 'head', axis=0, tiled=True)]
    all_to_all x0 -> x1, blocking collectives: none -> 58.3 us  [local(): lax.all_to_all(d_attn, 'head', split_axis=1, concat_axis=0, tiled=True)]
    all_gather x1, waiting for transfers between devices: 0.01 us -> 38.8 us  [local(): whole_weight = lax.all_gather(w_kv, 'dp', axis=0, tiled=True)]
    unnamed x17 -> x21, local copies, waits for them, and re-layouts: 23.4 us -> 24 us
    unnamed x5 -> x4, waiting for transfers between devices: 81.9 us -> 81.5 us
  transfers between devices with their start and end apart: 7 -> 6, of which waited for: 4 -> 5; matrix products, arithmetic and copies ran while one was open for 7% -> 7% of each run, Pallas kernels for 0% -> 0%
where the time goes in v1:
time: 765 us; the launch traced here: 760 us
  waiting for transfers between devices  317 us (41%)
  matrix products  237 us (31%)
  local copies, waits for them, and re-layouts  99.1 us (13%)
  blocking collectives  58.3 us (8%)
  between operations  13.9 us (2%)
  starting transfers between devices  13.8 us (2%)
  loops' own time  11.1 us (1%)
  other arithmetic  10.1 us (1%)
    psum x1, waiting for transfers between devices, local(): lax.psum(head_terms.astype(jnp.bfloat16), 'head').astype(jnp.float32)  143 us
    unnamed x4, waiting for transfers between devices  81.5 us
    all_to_all x1, blocking collectives, local(): lax.all_to_all(d_attn, 'head', split_axis=1, concat_axis=0, tiled=True)  58.3 us
    dot_general x16, matrix products, one_block(): jnp.einsum('hqk,qhd->khd', probs_low, out_rows, preferred_element_type=jn...  52.8 us
    all_to_all x1, waiting for transfers between devices, local(): latents = jnp.concatenate(lax.all_to_all(y1, 'head', 0, 0), 0)  50.2 us
    dot_general x16, matrix products, one_block(): jnp.einsum('hqk,qhd->khd', dscore_low, query_rows, preferred_element_type...  49.7 us
    all_gather x1, waiting for transfers between devices, local(): whole_weight = lax.all_gather(w_kv, 'dp', axis=0, tiled=True)  38.8 us
    dot_general x16, matrix products, one_block(): jnp.einsum('hqk,khd->qhd', dscore_low, key_rows, preferred_element_type=j...  34.8 us
  transfers between devices with their start and end apart: 6, of which 5 were waited for; matrix products, arithmetic and copies ran while one was open for 7% of the time, Pallas kernels for 0%

profile of v1, /device:TPU:2, one launch (start us, length us, event | category | flops | bytes accessed | tf_op | source)
XLA Modules:
  0.0 760.2 jit_solution(4930533409590585234)
XLA Ops:
  10.4 58.3 %all_to_all.56 = bf16[128,16,512]{0,2,1:T(8,128)(2,1)} all-to-all(bf16[128,16,512]{0,2,1:T(8,128)(2,1)S(1)} %bitcast.79), channel_id=1, replica_groups=mesh['dp'=16,'head'=16] {'head'}, dimensions={1} | all-to-all | bytes 4194304 | tf_op jit(solution)/shard_map/all_to_all | solution.py:98
  70.5 4.2 all-to-all-start.1
  74.8 4.6 copy.51
  79.4 50.2 %all-to-all-done.1 = bf16[16,128,576]{1,2,0:T(8,128)(2,1)S(1)} async-done(((bf16[16,128,576]{1,2,0:T(8,128)(2,1)}), bf16[16,128,576]{1,2,0:T(8,128)(2,1)S(1)}, u32[]{:S(2)}, u32[]{:S(2)}) %all-to-all-start.1) | async-done | bytes 2359328 | tf_op jit(solution)/shard_map/all_to_all | solution.py:101
  131.1 4.6 all-to-all-start
  136.8 4.3 copy.55
  141.1 4.2 reshape.123
  148.8 38.8 %all-gather.2.cloned.1.call-done = bf16[512,1024]{1,0:T(8,128)(2,1)} async-done(((bf16[32,1024]{1,0:T(8,128)(2,1)}), bf16[512,1024]{1,0:T(8,128)(2,1)}) %all-gather.2.cloned.1.call-update) | async-done | bytes 1048592 | tf_op jit(solution)/shard_map/all_gather | solution.py:103
  187.6 4.2 convolution_convert_fusion
  194.4 4.0 copy.68
  198.4 3.4 concatenate.23
  203.9 3.6 all-to-all-done
  207.5 3.7 copy.52
  211.2 5.8 reshape.118
  217.0 3.5 broadcast_in_dim.54
  223.1 266.0 %while.16 = (s32[]{:T(128)}, f32[2432,4,192]{0,2,1:T(8,128)}, f32[2432,4,128]{0,2,1:T(8,128)}, bf16[16,128,4,192]{1,3,2,0:T(8,128)(2,1)}, s32[16]{0:T(128)S(1)},...) while((s32[]{:T(128)}, f32[2432,4,192]{0,2,1:T(8,128)}, ...), condition=%wide.region_6.7_spmd, body=%wide.region_2.6_spmd.sunk | while | flops 711002240 | bytes 15294786 | solution.py:84
  350.6 3.3 fusion.129
  450.3 3.3 fusion.129
  489.0 4.7 copy.58
  493.7 4.8 all-to-all-start.3
  510.7 6.3 fusion.67
  519.3 142.8 %all-reduce.5.cloned.1.call-done = bf16[2048,576]{0,1:T(8,128)(2,1)} async-done(((bf16[2048,576]{0,1:T(8,128)(2,1)}), bf16[2048,576]{0,1:T(8,128)(2,1)}) %all-reduce.5.cloned.1.call-update) | async-done | bytes 2359312 | tf_op jit(solution)/shard_map/psum | solution.py:140
  663.7 80.8 %reduce-scatter.4.cloned.1.call-done = bf16[32,1024]{1,0:T(8,128)(2,1)} async-done(((bf16[512,1024]{1,0:T(8,128)(2,1)}), bf16[32,1024]{1,0:T(8,128)(2,1)}) %reduce-scatter.4.cloned.1.call-update) | async-done | bytes 65552
  749.1 4.6 copy.60
  (252 shorter events, 287.1 us)
Async XLA Ops:
  10.4 58.3 %copy-start.4 = (bf16[128,576]{0,1:T(8,128)(2,1)S(1)}, bf16[128,576]{0,1:T(8,128)(2,1)}, u32[]{:S(2)}) copy-start(bf16[128,576]{0,1:T(8,128)(2,1)} %param.8) | copy-start | bytes 442372
  70.5 59.1 %all-to-all-start.1 = ((bf16[16,128,576]{1,2,0:T(8,128)(2,1)}), bf16[16,128,576]{1,2,0:T(8,128)(2,1)S(1)}, u32[]{:S(2)}, u32[]{:S(2)}) async-start(bf16[16,128,576]{1,2,0:T(8,128)(2,1)} %stack.2), calls=%async_computation.1 | async-start | bytes 4718592 | tf_op jit(solution)/shard_map/all_to_all | solution.py:101
  129.6 1.4 copy-start
  129.6 6.8 copy-start.6
  131.1 76.5 %all-to-all-start = ((bf16[128,16,768]{0,2,1:T(8,128)(2,1)}), bf16[128,16,768]{0,2,1:T(8,128)(2,1)S(1)}, u32[]{:S(2)}, u32[]{:S(2)}) async-start(bf16[128,16,768]{0,2,1:T(8,128)(2,1)} %bitcast.7), calls=%async_computation | async-start | bytes 6291456 | tf_op jit(solution)/shard_map/all_to_all | solution.py:97
  135.7 51.9 %all-gather.2.cloned.1.call-start = ((), (), s32[]{:S(2)}) async-start(), calls=%async_computation.5 | async-start | bytes 1114112 | tf_op jit(solution)/shard_map/all_gather | solution.py:103
  147.3 1.4 copy-start.3
  198.4 3.4 slice-start
  198.4 3.5 copy-start.1
  493.7 252.6 %all-to-all-start.3 = ((bf16[16,128,768]{2,1,0:T(8,128)(2,1)}), bf16[16,128,768]{2,1,0:T(8,128)(2,1)S(1)}, u32[]{:S(2)}, u32[]{:S(2)}) async-start(bf16[16,128,768]{2,1,0:T(8,128)(2,1)} %copy.58), calls=%async_computation.3 | async-start | bytes 6291456 | tf_op jit(solution)/shard_map/all_to_all | solution.py:125
  498.5 163.6 %all-reduce.5.cloned.1.call-start = ((), (), s32[]{:S(2)}) async-start(), calls=%async_computation.6 | async-start | bytes 4718592 | tf_op jit(solution)/shard_map/psum | solution.py:140
  505.3 1.2 copy-start.5
  505.9 3.0 copy-start.2
  510.6 233.8 %reduce-scatter.4.cloned.1.call-start = ((), (), s32[]{:S(2)}) async-start(), calls=%async_computation.7 | async-start | bytes 1114112
Sparse Core Ops, SparseCore 0:
  139.0 48.6 all-gather.1
  510.8 151.2 all-reduce.4
  665.6 78.8 reduce-scatter.3
